TPU v7x, 32 devices: a whole 2x2x4 slice. The times are simulated.
32 devices in a mesh: node: 8 (over z, x), feat: 4 (over y, core).
Axes of the slice: x: 2, y: 2, z: 4, core: 2. Of those that a mesh axis runs over, the one named last changes fastest.
Arguments:
- feature_table: bfloat16 [8192, 2048], P('node', 'feat'), may hold values from -6 to 6
- hub_table: bfloat16 [32, 2048], P('node', 'feat'), may hold values from -6 to 6
- first_self: bfloat16 [2048, 2048], P('feat'), may hold values from -0.125 to 0.125
- first_pooled: bfloat16 [2048, 2048], P('feat'), may hold values from -0.125 to 0.125
- second_self: bfloat16 [2048, 256], P('feat'), may hold values from -0.125 to 0.125
- second_pooled: bfloat16 [2048, 256], P('feat'), may hold values from -0.125 to 0.125
- first_lists: int32 [3072, 10], P('node'), may hold values from 0 to 8223, as said below
- first_counts: int32 [3072], P('node'), may hold values from 1 to 10
- second_lists: int32 [2048, 5], P('node'), may hold values from 0 to 3071, as said below
- second_counts: int32 [2048], P('node'), may hold values from 1 to 5
Outputs:
- embedding: bfloat16 [2048, 256], P(('node', 'feat'))
Inputs may be any that keep to these rules, and one draw needn't show every extreme that they name: `first_lists`: an entry below 8192 names a row of feature_table, held by node shard (entry // 1024); an entry v of 8192 or more names hub clip v - 8192, owned by node shard (v - 8192) // 4. Slots at or beyond a clip's count are padding and still hold such entries. Of the 3840 entries of one node shard's rows, padding included, at most 480 name feature rows held by any one node shard; in every draw one node shard is named exactly 480 times by the rows of every node shard. `second_lists`: entries name frontier clips, held by node shard (entry // 384). Of the 1280 entries of one node shard's rows, padding included, exactly 160 name frontier clips of each node shard.
All inputs are finite; a program needn't handle non-finite values.
Results may differ from a plain program's by a relative error of at most 0.0052.
Values may be sent and summed in bfloat16 or wider, within the bound.
A program may use at most 64 MiB of HBM per device.

v0:
```python
import functools

import jax
import jax.numpy as jnp
from jax import lax
from jax.experimental import pallas as pl
from jax.experimental.pallas import tpu as pltpu
from jax.sharding import PartitionSpec as P

MESH = pl.DeviceIdType.MESH
CORES = 2


def greet(peers):
    barrier = pltpu.get_barrier_semaphore()
    for peer in peers:
        pl.semaphore_signal(barrier, inc=1, device_id=peer, device_id_type=MESH)
    pl.semaphore_wait(barrier, len(peers))


def remote(src, dst, sends, recvs, peer):
    return pltpu.make_async_remote_copy(
        src_ref=src, dst_ref=dst, send_sem=sends, recv_sem=recvs, device_id=peer, device_id_type=MESH
    )


def count_tiles(local, fan, width, store):
    rows = local.shape[0]
    local = local.astype(jnp.int16)
    one, zero = jnp.bfloat16(1), jnp.bfloat16(0)
    for start in range(0, width, 128):
        columns = (lax.broadcasted_iota(jnp.int32, (rows, 128), 1) + start).astype(jnp.int16)
        total = jnp.zeros((rows, 128), jnp.bfloat16)
        for k in range(fan):
            picked = jnp.broadcast_to(local[:, k : k + 1], (rows, 128))
            total = total + jnp.where(picked == columns, one, zero)
        store(start, total)


def main_kernel(
    sizes,
    table_ref,
    hub_ref,
    self_one,
    pool_one,
    self_two,
    pool_two,
    packed_ref,
    counts_ref,
    out_ref,
    lists,
    local,
    tables,
    matrix,
    matrix_two,
    weights,
    means,
    acc,
    z_send,
    z_recv,
    part,
    c_send,
    c_recv,
    y_send,
    y_recv,
    own_ref,
    mixed,
    mc_send,
    mc_recv,
    my_send,
    my_recv,
    mx_send,
    mx_recv,
    acc_z,
    mz_send,
    mz_recv,
    n_ss,
    n_rs,
    x_ss,
    x_rs,
    h_ss,
    h_rs,
    z_ss,
    z_rs,
    c_ss,
    c_rs,
    y_ss,
    y_rs,
    mc_ss,
    mc_rs,
    my_ss,
    my_rs,
    mx_ss,
    mx_rs,
    mz_ss,
    mz_rs,
):
    big_z, big_x, big_y, fan_one, fan_two, hubs_here, edges = sizes
    f32, bf16 = jnp.float32, jnp.bfloat16
    node = lax.axis_index("node")
    feat = lax.axis_index("feat")
    z, x = node // big_x, lax.rem(node, big_x)
    y, core = feat // CORES, lax.rem(feat, CORES)
    x_peers = [{"node": z * big_x + lax.rem(x + o, big_x)} for o in range(1, big_x)]
    z_peers = [{"node": lax.rem(z + o, big_z) * big_x + x} for o in range(1, big_z)]
    y_peers = [{"feat": lax.rem(y + o, big_y) * CORES + core} for o in range(1, big_y)]
    other = 1 - core
    c_peer = {"feat": y * CORES + other}
    shards = big_z * big_x
    n_peers = [{"node": lax.rem(node + o, shards)} for o in range(1, shards)]
    greet(n_peers + y_peers + [c_peer])

    rows, width = table_ref.shape
    front = acc.shape[0]
    reach = tables.shape[1]
    halves = len(edges) - 1

    list_copies = []
    for o, peer in enumerate(n_peers):
        copy = remote(packed_ref, lists.at[node], n_ss.at[o], n_rs.at[o], peer)
        copy.start()
        list_copies.append(copy)
    table_copies = []
    for h in range(halves):
        cut = pl.ds(edges[h], edges[h + 1] - edges[h])
        for o, peer in enumerate(x_peers):
            copy = remote(
                table_ref.at[:, cut],
                tables.at[1 + o, pl.ds(0, rows), cut],
                x_ss.at[h, o],
                x_rs.at[h, o],
                peer,
            )
            copy.start()
            table_copies.append(copy)
        if h == 0:
            for o, peer in enumerate(x_peers):
                copy = remote(
                    hub_ref,
                    tables.at[1 + o, pl.ds(rows, hub_ref.shape[0])],
                    h_ss.at[o],
                    h_rs.at[o],
                    peer,
                )
                copy.start()
                table_copies.append(copy)
    first_copies = 2 * len(x_peers)
    lists[node] = packed_ref[...]
    tail = rows + hub_ref.shape[0]
    tables[0, 0:rows] = table_ref[...]
    tables[0, rows:tail] = hub_ref[...]
    for slot in range(big_x):
        tables[slot, tail:reach] = jnp.zeros((reach - tail, width), bf16)
    for copy in list_copies:
        copy.wait()

    def decode(n, carry):
        entry = lists[n]
        found = jnp.full(entry.shape, -1, jnp.int32)
        for slot in range(big_x):
            owner = z * big_x + lax.rem(x - slot + big_x, big_x)
            feature_at = entry - owner * rows
            hub_at = entry - shards * rows - owner * hubs_here
            found = jnp.where(
                (feature_at >= 0) & (feature_at < rows), feature_at + slot * reach, found
            )
            found = jnp.where(
                (hub_at >= 0) & (hub_at < hubs_here), hub_at + (slot * reach + rows), found
            )
        line = lax.broadcasted_iota(jnp.int32, entry.shape, 0)
        seconds = jnp.clip(entry - node * front, -1, front)
        seconds = jnp.where(line == fan_one + fan_two, entry, seconds)
        local[n] = jnp.where(line < fan_one, found, seconds).T
        return carry

    lax.fori_loop(0, shards, decode, 0)

    def fill(target, at):
        def step(i, carry):
            row0 = pl.multiple_of(i * 32, 32)

            def store(start, value):
                matrix[at, pl.ds(row0, 32), start : start + 128] = value

            count_tiles(local[target, pl.ds(row0, 32), :], fan_one, reach * big_x, store)
            return carry

        lax.fori_loop(0, front // 32, step, 0)

    def sums_of(at, top, deep, low, high):
        total = jnp.dot(matrix[at, top : top + deep, 0:reach], tables[0, :, low:high], preferred_element_type=f32)
        for slot in range(1, big_x):
            total = total + jnp.dot(
                matrix[at, top : top + deep, slot * reach : (slot + 1) * reach],
                tables[slot, :, low:high],
                preferred_element_type=f32,
            )
        return total

    half = front // 2
    pieces = [(h, 0, front, edges[h], edges[h + 1]) for h in range(halves)]
    if halves > 1:
        last = pieces.pop()
        pieces += [(last[0], r * half, half, last[3], last[4]) for r in range(2)]

    def z_copy(p, s, to):
        peer = {"node": to * big_x + x}
        _, top, deep, low, high = pieces[p]
        at = (s, pl.ds(top, deep), pl.ds(low, high - low))
        return remote(z_send.at[at], z_recv.at[at], z_ss.at[p, s], z_rs.at[p, s], peer)

    slots = matrix.shape[0]
    fill(lax.rem(z + 1, big_z) * big_x + x, 0)
    for copy in table_copies[:first_copies]:
        copy.wait()

    def first_half(s, carry):
        zt = lax.rem(z + 1 + s, big_z)
        at = lax.rem(s, slots)

        @pl.when(s > 0)
        def _():
            fill(zt * big_x + x, at)

        z_send[s, :, 0 : edges[1]] = sums_of(at, 0, front, 0, edges[1]).astype(bf16)
        z_copy(0, s, zt).start()
        return carry

    lax.fori_loop(0, big_z - 1, first_half, 0)
    for p in range(1, len(pieces)):
        h, top, deep, low, high = pieces[p]
        if top == 0:
            begin = first_copies + (h - 1) * len(x_peers)
            for copy in table_copies[begin : begin + len(x_peers)]:
                copy.wait()

        def other_piece(s, carry, p=p, top=top, deep=deep, low=low, high=high):
            z_send[s, top : top + deep, low:high] = sums_of(s, top, deep, low, high).astype(bf16)
            z_copy(p, s, lax.rem(z + 1 + s, big_z)).start()
            return carry

        lax.fori_loop(0, big_z - 1, other_piece, 0)
    fill(node, 0)
    acc[...] = sums_of(0, 0, front, 0, width)

    hidden_part = part.shape[2]
    feats = big_y * CORES

    def own_part(f, carry):
        at = pl.ds(pl.multiple_of(f * hidden_part, 128), hidden_part)
        part[f] = jnp.dot(table_ref[0:front, :], self_one[:, at], preferred_element_type=f32)
        return carry

    lax.fori_loop(0, feats, own_part, 0)

    piece = out_ref.shape[0]

    def fill_two(at, carry):
        n, f = at // feats, lax.rem(at, feats)
        zz, xx = n // big_x, lax.rem(n, big_x)
        yy, cc = f // CORES, lax.rem(f, CORES)
        to = (((cc * big_y + yy) * big_x + xx) * big_z + zz) * piece
        from_row = pl.multiple_of(f * piece, 16)
        to_row = pl.multiple_of(to, 16)
        block = local[n, pl.ds(from_row, piece), :]

        def store(start, value):
            matrix_two[pl.ds(to_row, piece), start : start + 128] = value

        count_tiles(block[:, fan_one : fan_one + fan_two], fan_two, front, store)
        weights[pl.ds(to_row, piece), :] = 1.0 / block[
            :, fan_one + fan_two : fan_one + fan_two + 1
        ].astype(f32)
        return carry

    lax.fori_loop(0, shards * feats, fill_two, 0)

    def c_copy(r, s):
        at = (s, pl.ds(r * half, half))
        return remote(c_send.at[at], c_recv.at[at], c_ss.at[r, s], c_rs.at[r, s], c_peer)

    def y_copy(r, s, to):
        peer = {"feat": to * CORES + core}
        at = (s, pl.ds(r * half, half))
        return remote(y_send.at[at], y_recv.at[at], y_ss.at[r, s], y_rs.at[r, s], peer)

    for r in range(2):
        top, end = r * half, (r + 1) * half
        for p, (_, first, deep, low, high) in enumerate(pieces):
            if first == top:
                for s in range(big_z - 1):
                    z_copy(p, s, lax.rem(z + 1 + s, big_z)).wait()
                    acc[first : first + deep, low:high] += z_recv[
                        s, first : first + deep, low:high
                    ].astype(f32)
        means[top:end, :] = (acc[top:end, :] / counts_ref[top:end, :].astype(f32)).astype(bf16)

        def part_of(f, top=top, end=end):
            at = pl.ds(pl.multiple_of(f * hidden_part, 128), hidden_part)
            return part[f, top:end, :] + jnp.dot(
                means[top:end, :], pool_one[:, at], preferred_element_type=f32
            )

        def c_phase(s, carry, r=r, top=top, end=end, part_of=part_of):
            yt = lax.rem(y + 1 + s, big_y)
            c_send[s, top:end, :] = part_of(yt * CORES + other).astype(bf16)
            c_copy(r, s).start()
            return carry

        lax.fori_loop(0, big_y, c_phase, 0)

        def y_step(s, carry, r=r, top=top, end=end, part_of=part_of):
            yt = lax.rem(y + 1 + s, big_y)
            total = part_of(yt * CORES + core)
            c_copy(r, s).wait()
            total = total + c_recv[s, top:end, :].astype(f32)

            @pl.when(s < big_y - 1)
            def _():
                y_send[s, top:end, :] = total.astype(bf16)
                y_copy(r, s, yt).start()

            @pl.when(s == big_y - 1)
            def _():
                part[0, top:end, :] = total

            return carry

        lax.fori_loop(0, big_y, y_step, 0)
    total = part[0]
    for s in range(big_y - 1):
        for r in range(2):
            y_copy(r, s, lax.rem(y + 1 + s, big_y)).wait()
        total = total + y_recv[s].astype(f32)
    hidden = jnp.maximum(total, 0.0).astype(bf16)

    projected = jnp.dot(hidden, pool_two[...], preferred_element_type=f32).astype(bf16)
    own_ref[...] = jnp.dot(hidden[0 : piece * feats], self_two[...], preferred_element_type=f32)
    quarter = big_x * big_z * piece
    slab = big_z * piece

    def mix(k, s, c, yy):
        at = pl.ds(pl.multiple_of((c * big_y + yy) * quarter, 16), quarter)
        mixed[k, s] = (
            jnp.dot(matrix_two[at, :], projected, preferred_element_type=f32) * weights[at, :]
        )
        row = pl.multiple_of((x * big_z + z) * piece, 16)
        from_row = pl.multiple_of((yy * CORES + c) * piece, 16)
        mixed[k, s, pl.ds(row, piece), :] += own_ref[pl.ds(from_row, piece), :]

    core_copies = []
    for s in range(big_y):
        mix(0, s, other, lax.rem(y + 1 + s, big_y))
        mc_send[s] = mixed[0, s].astype(bf16)
        copy = remote(mc_send.at[s], mc_recv.at[s], mc_ss.at[s], mc_rs.at[s], c_peer)
        copy.start()
        core_copies.append(copy)
    for s in range(big_y):
        mix(1, s, core, lax.rem(y + 1 + s, big_y))
    x_rows = [
        pl.ds(pl.multiple_of(lax.rem(x + 1 + o, big_x) * slab, 16), slab) for o in range(big_x)
    ]
    y_copies = {}
    for s in range(big_y):
        core_copies[s].wait()
        mixed[1, s] += mc_recv[s].astype(f32)
        if s < big_y - 1:
            for o in range(big_x):
                my_send[s, o] = mixed[1, s, x_rows[o], :].astype(bf16)
                copy = remote(
                    my_send.at[s, o], my_recv.at[s, o], my_ss.at[s, o], my_rs.at[s, o], y_peers[s]
                )
                copy.start()
                y_copies[s, o] = copy
    x_copies = []
    for o in range(big_x):
        total = mixed[1, big_y - 1, x_rows[o], :]
        for s in range(big_y - 1):
            y_copies[s, o].wait()
            total = total + my_recv[s, o].astype(f32)
        if o < big_x - 1:
            mx_send[o] = total.astype(bf16)
            copy = remote(mx_send.at[o], mx_recv.at[o], mx_ss.at[o], mx_rs.at[o], x_peers[o])
            copy.start()
            x_copies.append(copy)
    for o, copy in enumerate(x_copies):
        copy.wait()
        total = total + mx_recv[o].astype(f32)
    acc_z[...] = total
    mz_send[...] = total.astype(bf16)
    z_copies = []
    for o in range(big_z - 1):
        row = pl.multiple_of(lax.rem(z + 1 + o, big_z) * piece, 16)
        copy = remote(
            mz_send.at[pl.ds(row, piece)], mz_recv.at[o], mz_ss.at[o], mz_rs.at[o], z_peers[o]
        )
        copy.start()
        z_copies.append(copy)
    total = acc_z[pl.ds(pl.multiple_of(z * piece, 8), piece), :]
    for o, copy in enumerate(z_copies):
        copy.wait()
        total = total + mz_recv[o].astype(f32)
    scale = lax.rsqrt(jnp.mean(total * total, axis=1, keepdims=True) + 1e-06)
    out_ref[...] = (total * scale).astype(bf16)


def body(
    feature_table,
    hub_table,
    first_self,
    first_pooled,
    second_self,
    second_pooled,
    first_lists,
    first_counts,
    second_lists,
    second_counts,
):
    shards = lax.axis_size("node")
    feats = lax.axis_size("feat")
    big_x = 2 ** ((shards.bit_length() - 1) // 2)
    big_z = shards // big_x
    big_y = feats // CORES
    rows_here, width = feature_table.shape
    hubs_here = hub_table.shape[0]
    front, fan_one = first_lists.shape
    targets_here, fan_two = second_lists.shape
    piece = targets_here // feats
    out_width = second_self.shape[1]
    hidden_part = second_self.shape[0]

    slots_one = jnp.arange(fan_one, dtype=jnp.int32)[None, :]
    slots_two = jnp.arange(fan_two, dtype=jnp.int32)[None, :]
    lists_one = jnp.where(slots_one < first_counts[:, None], first_lists, -1).T
    lists_two = jnp.where(slots_two < second_counts[:, None], second_lists, -1).T
    lists_two = jnp.concatenate([lists_two, second_counts[None, :]], axis=0)
    lists_two = jnp.pad(lists_two, ((0, 0), (0, front - targets_here)))
    packed = jnp.concatenate([lists_one, lists_two], axis=0)
    hubs = jnp.pad(hub_table, ((0, -hubs_here % 16), (0, 0)))
    reach = rows_here + 128
    edges = (0, 128, 256, width) if width > 256 else (0, width)
    chunks = len(edges) if len(edges) > 2 else 1
    bf16, f32 = jnp.bfloat16, jnp.float32
    dma = pltpu.SemaphoreType.DMA
    zs, xs, ys = big_z - 1, big_x - 1, big_y - 1
    quarter = big_x * big_z * piece
    slab = big_z * piece
    block = (front, width)
    hblock = (front, hidden_part)
    vmem = pl.BlockSpec(memory_space=pltpu.VMEM)
    return pl.pallas_call(
        functools.partial(main_kernel, (big_z, big_x, big_y, fan_one, fan_two, hubs_here, edges)),
        out_shape=jax.ShapeDtypeStruct((piece, out_width), bf16),
        in_specs=[vmem] * 8,
        out_specs=vmem,
        scratch_shapes=[
            pltpu.VMEM((shards,) + packed.shape, jnp.int32),
            pltpu.VMEM((shards, front, packed.shape[0]), jnp.int32),
            pltpu.VMEM((big_x, reach, width), bf16),
            pltpu.VMEM((zs if chunks > 1 else 1, front, big_x * reach), bf16),
            pltpu.VMEM((targets_here * shards, front), bf16),
            pltpu.VMEM((targets_here * shards, 1), f32),
            pltpu.VMEM(block, bf16),
            pltpu.VMEM(block, f32),
            pltpu.VMEM((zs,) + block, bf16),
            pltpu.VMEM((zs,) + block, bf16),
            pltpu.VMEM((feats,) + hblock, f32),
            pltpu.VMEM((big_y,) + hblock, bf16),
            pltpu.VMEM((big_y,) + hblock, bf16),
            pltpu.VMEM((ys,) + hblock, bf16),
            pltpu.VMEM((ys,) + hblock, bf16),
            pltpu.VMEM((targets_here, out_width), f32),
            pltpu.VMEM((CORES, big_y, quarter, out_width), f32),
            pltpu.VMEM((big_y, quarter, out_width), bf16),
            pltpu.VMEM((big_y, quarter, out_width), bf16),
            pltpu.VMEM((ys, big_x, slab, out_width), bf16),
            pltpu.VMEM((ys, big_x, slab, out_width), bf16),
            pltpu.VMEM((xs, slab, out_width), bf16),
            pltpu.VMEM((xs, slab, out_width), bf16),
            pltpu.VMEM((slab, out_width), f32),
            pltpu.VMEM((slab, out_width), bf16),
            pltpu.VMEM((zs, piece, out_width), bf16),
            dma((shards - 1,)),
            dma((shards - 1,)),
            dma((len(edges) - 1, xs)),
            dma((len(edges) - 1, xs)),
            dma((xs,)),
            dma((xs,)),
            dma((chunks, zs)),
            dma((chunks, zs)),
            dma((2, big_y)),
            dma((2, big_y)),
            dma((2, ys)),
            dma((2, ys)),
            dma((big_y,)),
            dma((big_y,)),
            dma((ys, big_x)),
            dma((ys, big_x)),
            dma((xs,)),
            dma((xs,)),
            dma((zs,)),
            dma((zs,)),
        ],
        compiler_params=pltpu.CompilerParams(
            collective_id=1, has_side_effects=True, vmem_limit_bytes=60 * 1024 * 1024
        ),
    )(
        feature_table,
        hubs,
        first_self,
        first_pooled,
        second_self,
        second_pooled,
        packed,
        first_counts[:, None],
    )


def solution(mesh):
    return jax.shard_map(
        body,
        mesh=mesh,
        in_specs=(
            P("node", "feat"),
            P("node", "feat"),
            P("feat", None),
            P("feat", None),
            P("feat", None),
            P("feat", None),
            P("node", None),
            P("node"),
            P("node", None),
            P("node"),
        ),
        out_specs=P(("node", "feat"), None),
        check_vma=False,
    )
```

profile of v0, /device:TPU:0, one launch (start us, length us, event | category | flops | bytes accessed | tf_op | source)
XLA Modules:
  0.0 87.9 jit_solution(13271768093028883145)
XLA Ops:
  0.0 0.7 select_bitcast_fusion.1
  0.7 0.7 pad_add_fusion.1
  1.4 1.3 %pad.8.hub_ref = bf16[16,512]{1,0:T(8,128)(2,1)} pad(bf16[4,512]{1,0:T(4,128)(2,1)} %param.11, bf16[]{:T(256)} %constant.1.clone.1), padding=0_12x0_0 | pad | bytes 20482 | tf_op jit(solution)/shard_map/jit(_pad)/pad | solution.py:439
  2.7 0.7 select_bitcast_fusion
  3.4 0.6 pad_add_fusion.packed_ref
  4.0 1.5 %broadcast_in_dim.22.counts_ref = s32[384,1]{1,0:T(8,128)} reshape(s32[384]{0:T(512)} %param.17) | data formatting | bytes 3072 | tf_op jit(solution)/shard_map/broadcast_in_dim | solution.py:434
  5.5 81.0 %shard_map.100 = bf16[64,256]{1,0:T(8,128)(2,1)} custom-call(bf16[1024,512]{1,0:T(8,128)(2,1)} %table_ref.1, bf16[16,512]{1,0:T(8,128)(2,1)} %pad.8.hub_ref, bf16[512,2048]{1,0:T(8,128)(2,1)} %self_one.1, bf16[512,2048]{1,0:T(8,128)(2,1)} %pool_one.1, bf16[512,256]{1,0:T(8,128)(2,1)} %self_two.1, bf16[512,256]{1,0:T(8,128)(2,1)} %pool_two.1, ...), custom_call_target="tpu_custom_call" | custom-call | tf_op jit(solution)/shard_map/pallas_call | solution.py:451
  86.5 1.4 %copy.13 = bf16[64,256]{1,0:T(8,128)(2,1)} copy(bf16[64,256]{1,0:T(8,128)(2,1)} %shard_map.100) | data formatting | bytes 65536
where the time goes:
time: 88.2 us; the launch traced here: 87.9 us
  Pallas kernels  81 us (92%)
  local copies, waits for them, and re-layouts  4.14 us (5%)
  other arithmetic  2.75 us (3%)
    pallas_call x1, Pallas kernels, body(): pl.pallas_call(functools.partial(main_kernel, (big_z, big_x, big_y, fan_o...  81 us

commit v1 on v0

v1 whole, which is shorter than its diff:
```python
import functools
import types

import jax
import jax.numpy as jnp
from jax import lax
from jax.experimental import pallas as pl
from jax.experimental.pallas import tpu as pltpu
from jax.sharding import PartitionSpec as P

MESH = pl.DeviceIdType.MESH
CORES = 2
LANES = 128
TILES = 4
HUB_ROWS = 16
LIST_ROWS = 16


def greet(peers):
    barrier = pltpu.get_barrier_semaphore()
    for peer in peers:
        pl.semaphore_signal(barrier, inc=1, device_id=peer, device_id_type=MESH)
    pl.semaphore_wait(barrier, len(peers))


def remote(src, dst, sends, recvs, peer):
    return pltpu.make_async_remote_copy(
        src_ref=src, dst_ref=dst, send_sem=sends, recv_sem=recvs, device_id=peer, device_id_type=MESH
    )


def count_tiles(local, fan, names, store):
    rows = local.shape[0]
    local = local.astype(jnp.int16)
    one, zero = jnp.bfloat16(1), jnp.bfloat16(0)
    picked = [jnp.broadcast_to(local[:, k : k + 1], (rows, LANES)) for k in range(fan)]
    for at, columns in enumerate(names):
        columns = columns(rows)
        total = jnp.zeros((rows, LANES), jnp.bfloat16)
        for k in range(fan):
            total = total + jnp.where(picked[k] == columns, one, zero)
        store(at * LANES, total)


def plain_names(base, count):
    def name(start, rows):
        return (lax.broadcasted_iota(jnp.int32, (rows, LANES), 1) + start).astype(jnp.int16)

    return [functools.partial(name, base + at * LANES) for at in range(count)]


def main_kernel(d, names, *refs):
    r = types.SimpleNamespace(**dict(zip(names, refs)))
    f32, bf16 = jnp.float32, jnp.bfloat16
    node, feat = lax.axis_index("node"), lax.axis_index("feat")
    z, x = node // d.big_x, lax.rem(node, d.big_x)
    y, core = feat // CORES, lax.rem(feat, CORES)
    other = 1 - core
    place = core * d.big_y + y
    x_peers = [{"node": z * d.big_x + lax.rem(x + o, d.big_x)} for o in range(1, d.big_x)]
    y_peers = [{"feat": lax.rem(y + o, d.big_y) * CORES + core} for o in range(1, d.big_y)]
    n_peers = [{"node": lax.rem(node + o, d.shards)} for o in range(1, d.shards)]
    f_peers = [{"feat": lax.rem(feat + o, d.feats)} for o in range(1, d.feats)]
    c_peer = {"feat": y * CORES + other}

    def z_peer(to):
        return {"node": to * d.big_x + x}

    my_rows = pl.ds(pl.multiple_of(x * d.rows, d.rows), d.rows)
    my_units = pl.ds(pl.multiple_of(feat * d.hidden_part, d.hidden_part), d.hidden_part)
    loads = [
        pltpu.make_async_copy(r.table, r.tables.at[my_rows], r.load.at[0]),
        pltpu.make_async_copy(r.self_one, r.w_self, r.load.at[1]),
        pltpu.make_async_copy(r.pool_one, r.w_pool, r.load.at[2]),
        pltpu.make_async_copy(r.self_two, r.v_self.at[my_units], r.load.at[3]),
        pltpu.make_async_copy(r.pool_two, r.v_pool.at[my_units], r.load.at[4]),
    ]
    for copy in loads:
        copy.start()
    hub_top = d.big_x * d.rows
    r.hubs[...] = jnp.zeros(r.hubs.shape, bf16)
    r.hubs[0 : d.hubs_here, :] = r.hub[...]
    r.tables[hub_top : d.depth, :] = jnp.zeros((d.depth - hub_top, d.width), bf16)
    my_hubs = pl.ds(pl.multiple_of(hub_top + x * HUB_ROWS, HUB_ROWS), HUB_ROWS)
    r.tables[my_hubs, :] = r.hubs[...]
    greet(n_peers + f_peers)

    def x_copy(h, o):
        cut = pl.ds(h * LANES, LANES)
        return remote(
            r.table.at[:, cut], r.tables.at[my_rows, cut], r.x_ss.at[h, o], r.x_rs.at[h, o], x_peers[o]
        )


    def h_copy(o):
        return remote(r.hubs, r.tables.at[my_hubs], r.h_ss.at[o], r.h_rs.at[o], x_peers[o])

    for o in range(d.big_x - 1):
        h_copy(o).start()
        x_copy(0, o).start()

    line = lax.broadcasted_iota(jnp.int32, (LIST_ROWS, d.front), 0)
    r.raw[...] = jnp.full((LIST_ROWS, d.front), -1, jnp.int32)
    r.raw[0 : d.fan_one, :] = r.lists_one[...]
    counts = jnp.broadcast_to(r.counts_one[...], (LIST_ROWS, d.front))
    entry = jnp.where(line < jnp.minimum(counts, d.fan_one), r.raw[...], -1)

    def decode(to):
        here = entry - to * (d.big_x * d.rows)
        found = jnp.where((here >= 0) & (here < hub_top), here, -1)
        for slot in range(d.big_x):
            hub = entry - (d.shards * d.rows + (to * d.big_x + slot) * d.hubs_here)
            found = jnp.where(
                (hub >= 0) & (hub < d.hubs_here), hub + (hub_top + slot * HUB_ROWS), found
            )
        return found

    def l_copy(o):
        to = lax.rem(z + o, d.big_z)
        return remote(
            r.l_send.at[o - 1], r.l_recv.at[z], r.l_ss.at[o - 1], r.l_rs.at[o - 1], z_peer(to)
        )

    for o in range(1, d.big_z):
        r.l_send[o - 1] = decode(lax.rem(z + o, d.big_z)).astype(jnp.int16)
        l_copy(o).start()

    def place_rows(slot, found):
        turned = found.T
        for to, start, _ in d.order:
            r.local[slot, to : to + d.step, :] = turned[start : start + d.step, :]

    own_slot = d.big_z - 1
    place_rows(own_slot, jnp.where(line == d.fan_one, counts, decode(z)))

    line_two = lax.broadcasted_iota(jnp.int32, (8, d.targets), 0)
    counts_two = jnp.broadcast_to(r.counts_two[...], (8, d.targets))
    r.raw_two[...] = jnp.full((8, d.targets), -1, jnp.int32)
    r.raw_two[0 : d.fan_two, :] = r.lists_two[...]
    second = jnp.where(line_two < jnp.minimum(counts_two, d.fan_two), r.raw_two[...], -1)
    second = jnp.where(line_two == d.fan_two, counts_two, second)
    r.s_send[...] = second
    r.s_recv[node] = second

    def s_copy(o):
        return remote(r.s_send, r.s_recv.at[node], r.s_ss.at[o], r.s_rs.at[o], n_peers[o])

    for o in range(d.shards - 1):
        s_copy(o).start()

    for h in range(1, d.chunks):
        for o in range(d.big_x - 1):
            x_copy(h, o).start()

    def v_copies(o):
        return [
            remote(r.self_two, r.v_self.at[my_units], r.v_ss.at[0, o], r.v_rs.at[0, o], f_peers[o]),
            remote(r.pool_two, r.v_pool.at[my_units], r.v_ss.at[1, o], r.v_rs.at[1, o], f_peers[o]),
        ]

    for o in range(d.feats - 1):
        for copy in v_copies(o):
            copy.start()

    own_rows = pl.ds(pl.multiple_of(x * d.rows, d.rows), d.front)

    def own_part(j, carry):
        cut = pl.ds(pl.multiple_of(j * d.tile, LANES), d.tile)
        value = jnp.dot(r.tables[own_rows, :], r.w_self[:, cut], preferred_element_type=f32)
        for to, start, _ in d.order:
            r.part[j, to : to + d.step, :] = value[start : start + d.step, :]
        return carry

    turn = 2 * z // d.big_z

    turns = max(d.big_z - 1, 1)

    def target_of(s):
        mirrored = z + turn * (d.big_z - 1 - 2 * z)
        back = (s + mirrored) // turns
        to = (1 - back) * (d.big_z - 1 - s) + back * (s + mirrored - turns)
        return to + turn * (d.big_z - 1 - 2 * to)

    for o in range(1, d.big_z):
        l_copy(o).wait()

    def take_list(s, carry):
        place_rows(s, r.l_recv[target_of(s)].astype(jnp.int32))
        return carry

    lax.fori_loop(0, d.big_z - 1, take_list, 0)

    tile_names = plain_names(0, d.depth // LANES)

    def fill(slot):
        def group(i, carry):
            row0 = pl.multiple_of(i * 32, 32)

            def store(start, value):
                r.matrix[slot, pl.ds(row0, 32), start : start + LANES] = value

            count_tiles(r.local[slot, pl.ds(row0, 32), :], d.fan_one, tile_names, store)
            return carry

        lax.fori_loop(0, d.front // 32, group, 0)

    last = d.chunks - 1
    block = d.feats * d.step
    split = [h for h in (last - 1, last) if h > 0 or h == last]
    pieces = [(0, d.front, h) for h in range(split[0])]
    whole = len(pieces)
    piece_of = {}
    for group in (range(d.blocks - 1), (d.blocks - 1,)):
        for h in split:
            for q in group:
                piece_of[q, h] = len(pieces)
                pieces.append((q * block, block, h))
    odd = lax.rem(z, 2)
    partner = z + 1 - 2 * odd

    def region(p):
        top, deep, h = pieces[p]
        return pl.ds(top, deep), pl.ds(h * LANES, LANES)

    def held(s):
        to = target_of(s)
        return ((odd == 1) & (to > z)) | ((odd == 0) & (to < z))

    def led(s):
        to = target_of(s)
        return ((odd == 0) & (to > z + 1)) | ((odd == 1) & (to < z - 1))

    def hop_copy(s, p, slot, peer):
        rows, cut = region(p)
        return remote(
            r.z_send.at[s, rows, cut],
            r.z_recv.at[slot, rows, cut],
            r.z_ss.at[s, p],
            r.z_rs.at[slot, p],
            z_peer(peer),
        )

    def led_copy(s, p):
        return hop_copy(s, p, d.big_z + target_of(s), partner)

    def final_copy(s, p):
        return hop_copy(s, p, z, target_of(s))

    def arrival(slot, p):
        rows, cut = region(p)
        at = r.z_recv.at[slot, rows, cut]
        return remote(at, at, r.z_rs.at[slot, p], r.z_rs.at[slot, p], z_peer(lax.rem(z + 1, d.big_z)))

    def relay(p):
        top, deep, h = pieces[p]
        rows = slice(top, top + deep)
        cut = slice(h * LANES, (h + 1) * LANES)

        def one(s, carry):
            @pl.when(held(s))
            def _():
                slot = d.big_z + target_of(s)
                arrival(slot, p).wait_recv()
                r.z_send[s, rows, cut] = (
                    r.hold[s, rows, cut] + r.z_recv[slot, rows, cut].astype(f32)
                ).astype(bf16)
                final_copy(s, p).start()

            return carry

        lax.fori_loop(0, d.big_z - 1, one, 0)

    def sums(h, s):
        cut = slice(h * LANES, (h + 1) * LANES)
        value = jnp.dot(r.matrix[s], r.tables[:, cut], preferred_element_type=f32)

        kept = held(s)

        @pl.when(kept)
        def _():
            r.hold[s, :, cut] = value

        @pl.when(jnp.logical_not(kept))
        def _():
            r.z_send[s, :, cut] = value.astype(bf16)

    def launch(s, p):
        @pl.when(led(s))
        def _():
            led_copy(s, p).start()

        @pl.when(jnp.logical_not(held(s) | led(s)))
        def _():
            final_copy(s, p).start()

    def send_all(ps):
        for p in ps:
            for s in range(d.big_z - 1):
                launch(s, p)

    def chunk(h):
        for o in range(d.big_x - 1):
            x_copy(h, o).wait()

        def one_target(s, carry):
            sums(h, s)
            if h < split[0]:
                launch(s, h)
            return carry

        lax.fori_loop(0, d.big_z - 1, one_target, 0)

    relayed = set()

    def relays(p):
        if d.big_z > 2 and p not in relayed:
            relayed.add(p)

            relay(p)

    def fill_second(n, carry):
        local = (r.s_recv[n]).T
        r.turned[...] = local
        mine = r.turned[pl.ds(pl.multiple_of(feat * d.piece, 8), d.piece), :]
        row = pl.multiple_of(n * d.piece, 16)

        def store(start, value):
            r.matrix_two[pl.ds(row, d.piece), start : start + LANES] = value

        found = jnp.clip(mine[:, 0 : d.fan_two] - node * d.front, -1, d.front)
        count_tiles(found, d.fan_two, second_names, store)
        r.scale_two[pl.ds(row, d.piece), :] = 1.0 / mine[:, d.fan_two : d.fan_two + 1].astype(f32)
        return carry

    def second_name(start, rows):
        lane = lax.broadcasted_iota(jnp.int32, (rows, LANES), 1) + start
        q = lane // block
        rest = lane - q * block
        spot = rest // d.step
        within = rest - spot * d.step
        c = spot // d.big_y
        f = (spot - c * d.big_y) * CORES + c
        early = d.targets + f * d.step + within
        late = f * d.piece + (q - 1) * d.step + within
        return jnp.where(q == 0, early, late).astype(jnp.int16)

    second_names = [functools.partial(second_name, at) for at in range(0, d.front, LANES)]

    fill(0)
    if d.big_z > 2:
        fill(1)
    for o in range(d.big_x - 1):
        x_copy(0, o).wait()
        h_copy(o).wait()
    loads[0].wait()

    def first_sums(s, carry):
        @pl.when(s > 1)
        def _():
            fill(s)

        sums(0, s)
        if split[0] > 0:
            launch(s, 0)
        return carry

    lax.fori_loop(0, d.big_z - 1, first_sums, 0)
    loads[1].wait()
    lax.fori_loop(0, TILES, own_part, 0)
    for h in range(1, d.chunks):
        if h < last - 1:
            relays(h - 1)
        chunk(h)
        if h == last - 1:
            if h > 0:
                send_all([piece_of[q, h] for q in range(d.blocks - 1)])
            if h - 1 >= 0 and split[0] > h - 1:
                relays(h - 1)
        if h == max(last - 2, 1):
            for o in range(d.shards - 1):
                s_copy(o).wait()
            lax.fori_loop(0, d.shards, fill_second, 0)
        if h == last - 1:
            fill(own_slot)
    if last <= 1:
        if last == 0:
            for o in range(d.shards - 1):
                s_copy(o).wait()
            lax.fori_loop(0, d.shards, fill_second, 0)
        fill(own_slot)
        send_all(range(whole, len(pieces)))
    else:
        send_all([piece_of[q, last] for q in range(d.blocks - 1)])
        send_all([piece_of[d.blocks - 1, h] for h in split])
    r.acc[...] = jnp.dot(r.matrix[own_slot], r.tables[...], preferred_element_type=f32)

    def gather(p):
        top, deep, h = pieces[p]
        rows = slice(top, top + deep)
        cut = slice(h * LANES, (h + 1) * LANES)
        for o in range(1, d.big_z):
            src = lax.rem(z + o, d.big_z)
            below = (src < z) & (lax.rem(src, 2) == 1)
            above = (src > z) & (lax.rem(src, 2) == 0)

            @pl.when((src == partner) | below | above)
            def _(src=src):
                arrival(src, p).wait_recv()
                r.acc[rows, cut] += r.z_recv[src, rows, cut].astype(f32)

    early = [piece_of[q, split[0]] for q in range(d.blocks - 1)] if len(split) > 1 else []
    for p in list(range(whole)) + early:
        relays(p)
    for p in range(whole):
        gather(p)
    loads[2].wait()
    half = d.big_y * d.step

    def c_copy(q, j):
        return remote(r.c_send.at[q, j], r.c_recv.at[q, j], r.c_ss.at[q, j], r.c_rs.at[q, j], c_peer)

    def y_copy(q, j, o):
        return remote(
            r.y_send.at[q, j, o], r.y_recv.at[q, j, o], r.y_ss.at[q, j, o], r.y_rs.at[q, j, o], y_peers[o]
        )

    def project(q):
        rows = slice(q * block, (q + 1) * block)
        counted = r.local[own_slot, rows, d.fan_one : d.fan_one + 1].astype(f32)
        r.means[rows, :] = (r.acc[rows, :] / counted).astype(bf16)

        def tile(j, carry):
            cut = pl.ds(pl.multiple_of(j * d.tile, LANES), d.tile)
            r.tot[...] = r.part[j, rows, :] + jnp.dot(
                r.means[rows, :], r.w_pool[:, cut], preferred_element_type=f32
            )
            far = pl.ds(pl.multiple_of(other * half, half), half)
            near = pl.ds(pl.multiple_of(core * half, half), half)
            r.c_send[q, j] = r.tot[far, :].astype(bf16)
            c_copy(q, j).start()
            r.mine[q, j] = r.tot[near, :].reshape(d.big_y, d.step, d.tile)
            return carry

        lax.fori_loop(0, TILES, tile, 0)

    def across(q):
        def tile(j, carry):
            c_copy(q, j).wait()
            r.mine[q, j] += r.c_recv[q, j].astype(f32).reshape(d.big_y, d.step, d.tile)
            for o in range(d.big_y - 1):
                r.y_send[q, j, o] = r.mine[q, j, lax.rem(y + 1 + o, d.big_y)].astype(bf16)
                y_copy(q, j, o).start()
            return carry

        lax.fori_loop(0, TILES, tile, 0)

    def p_copy(q, o):
        at = r.proj.at[pl.ds(pl.multiple_of(q * block + place * d.step, d.step), d.step)]
        return remote(at, at, r.p_ss.at[q, o], r.p_rs.at[q, o], f_peers[o])

    def finish(q):
        mine = slice(q * d.step, (q + 1) * d.step)
        for j in range(TILES):
            total = r.mine[q, j, y]
            for o in range(d.big_y - 1):
                y_copy(q, j, o).wait()
                total = total + r.y_recv[q, j, o].astype(f32)
            r.hidden[mine, j * d.tile : (j + 1) * d.tile] = jnp.maximum(total, 0.0)
        value = jnp.dot(r.hidden[mine, :].astype(bf16), r.v_pool[...], preferred_element_type=f32)
        at = pl.ds(pl.multiple_of(q * block + place * d.step, d.step), d.step)
        r.proj[at, :] = value.astype(bf16).astype(r.proj.dtype)
        for o in range(d.feats - 1):
            p_copy(q, o).start()

    for q in range(d.blocks):
        for h in split:
            if piece_of[q, h] not in early:
                relays(piece_of[q, h])
        if q > 0:
            across(q - 1)
        for h in split:
            gather(piece_of[q, h])
        project(q)
        if q == 0:
            loads[3].wait()
            loads[4].wait()
            for o in range(d.feats - 1):
                for copy in v_copies(o):
                    copy.wait()
        if q > 0:
            finish(q - 1)
    across(d.blocks - 1)
    finish(d.blocks - 1)
    own_two = jnp.dot(r.hidden[d.step :, :].astype(bf16), r.v_self[...], preferred_element_type=f32)
    for q in range(d.blocks):
        for o in range(d.feats - 1):
            p_copy(q, o).wait()
    r.mixed[...] = (
        jnp.dot(r.matrix_two[...], r.proj[...].astype(bf16), preferred_element_type=f32) * r.scale_two[...]
    )

    def m_copy(o):
        return remote(r.m_send.at[o], r.m_recv.at[o], r.m_ss.at[o], r.m_rs.at[o], n_peers[o])

    ways = sorted(range(d.shards - 1), key=lambda o: abs(o + 1 - d.shards // 2))
    for o in ways:
        to = pl.multiple_of(lax.rem(node + 1 + o, d.shards) * d.piece, 16)
        r.m_send[o] = r.mixed[pl.ds(to, d.piece), :].astype(bf16)
        m_copy(o).start()
    total = own_two + r.mixed[pl.ds(pl.multiple_of(node * d.piece, 16), d.piece), :]
    for s in range(d.big_z - 1):
        for p in range(len(pieces)):
            final_copy(s, p).wait_send()
    for o in reversed(ways):
        m_copy(o).wait()
        total = total + r.m_recv[o].astype(f32)
    scale = lax.rsqrt(jnp.mean(total * total, axis=1, keepdims=True) + 1e-06)
    r.out[...] = (total * scale).astype(bf16)


def body(
    feature_table,
    hub_table,
    first_self,
    first_pooled,
    second_self,
    second_pooled,
    first_lists,
    first_counts,
    second_lists,
    second_counts,
):
    d = types.SimpleNamespace()
    d.shards = lax.axis_size("node")
    d.feats = lax.axis_size("feat")
    d.big_x = 2 ** ((d.shards.bit_length() - 1) // 2)
    d.big_z = d.shards // d.big_x
    d.big_y = d.feats // CORES
    d.rows, d.width = feature_table.shape
    d.hubs_here = hub_table.shape[0]
    d.front, d.fan_one = first_lists.shape
    d.targets, d.fan_two = second_lists.shape
    d.piece = d.targets // d.feats
    d.out_width = second_self.shape[1]
    d.hidden_part = second_self.shape[0]
    units = d.hidden_part * d.feats
    d.tile = units // TILES
    d.depth = d.big_x * d.rows + -(-d.big_x * HUB_ROWS // LANES) * LANES
    d.chunks = d.width // LANES
    d.step = (d.front - d.targets) // d.feats
    d.blocks = d.front // (d.step * d.feats)
    assert d.step * d.feats * d.blocks == d.front and d.piece % d.step == 0
    order = []
    for q in range(d.blocks):
        for c in range(CORES):
            for yy in range(d.big_y):
                f = yy * CORES + c
                start = d.targets + f * d.step if q == 0 else f * d.piece + (q - 1) * d.step
                order.append((q * d.step * d.feats + (c * d.big_y + yy) * d.step, start, f))
    d.order = order
    bf16, f32, i32, i16 = jnp.bfloat16, jnp.float32, jnp.int32, jnp.int16
    dma, vm = pltpu.SemaphoreType.DMA, pltpu.VMEM
    zs, xs, ys, ns, fs = d.big_z - 1, d.big_x - 1, d.big_y - 1, d.shards - 1, d.feats - 1
    count = d.chunks * d.blocks
    half = d.big_y * d.step
    kind = bf16 if d.step % 16 == 0 else f32
    scratch = dict(
        tables=vm((d.depth, d.width), bf16),
        w_self=vm((d.width, units), bf16),
        w_pool=vm((d.width, units), bf16),
        v_self=vm((units, d.out_width), bf16),
        v_pool=vm((units, d.out_width), bf16),
        hubs=vm((HUB_ROWS, d.width), bf16),
        raw=vm((LIST_ROWS, d.front), i32),
        raw_two=vm((8, d.targets), i32),
        l_send=vm((zs, LIST_ROWS, d.front), i16),
        l_recv=vm((d.big_z, LIST_ROWS, d.front), i16),
        s_send=vm((8, d.targets), i32),
        s_recv=vm((d.shards, 8, d.targets), i32),
        turned=vm((d.targets, 8), i32),
        local=vm((d.big_z, d.front, LIST_ROWS), i32),
        matrix=vm((d.big_z, d.front, d.depth), bf16),
        matrix_two=vm((d.shards * d.piece, d.front), bf16),
        scale_two=vm((d.shards * d.piece, 1), f32),
        part=vm((TILES, d.front, d.tile), f32),
        hold=vm((zs, d.front, d.width), f32),
        z_send=vm((zs, d.front, d.width), bf16),
        z_recv=vm((2 * d.big_z, d.front, d.width), bf16),
        acc=vm((d.front, d.width), f32),
        means=vm((d.front, d.width), bf16),
        tot=vm((d.step * d.feats, d.tile), f32),
        mine=vm((d.blocks, TILES, d.big_y, d.step, d.tile), f32),
        c_send=vm((d.blocks, TILES, half, d.tile), bf16),
        c_recv=vm((d.blocks, TILES, half, d.tile), bf16),
        y_send=vm((d.blocks, TILES, ys, d.step, d.tile), bf16),
        y_recv=vm((d.blocks, TILES, ys, d.step, d.tile), bf16),
        hidden=vm((d.blocks * d.step, units), f32),
        proj=vm((d.front, d.out_width), kind),
        mixed=vm((d.shards * d.piece, d.out_width), f32),
        m_send=vm((ns, d.piece, d.out_width), bf16),
        m_recv=vm((ns, d.piece, d.out_width), bf16),
        load=dma((5,)),
        x_ss=dma((d.chunks, xs)),
        x_rs=dma((d.chunks, xs)),
        h_ss=dma((xs,)),
        h_rs=dma((xs,)),
        l_ss=dma((zs,)),
        l_rs=dma((zs,)),
        s_ss=dma((ns,)),
        s_rs=dma((ns,)),
        v_ss=dma((2, fs)),
        v_rs=dma((2, fs)),
        z_ss=dma((zs, count)),
        z_rs=dma((2 * d.big_z, count)),
        c_ss=dma((d.blocks, TILES)),
        c_rs=dma((d.blocks, TILES)),
        y_ss=dma((d.blocks, TILES, ys)),
        y_rs=dma((d.blocks, TILES, ys)),
        p_ss=dma((d.blocks, fs)),
        p_rs=dma((d.blocks, fs)),
        m_ss=dma((ns,)),
        m_rs=dma((ns,)),
    )
    inputs = ["table", "hub", "self_one", "pool_one", "self_two", "pool_two"]
    inputs += ["lists_one", "counts_one", "lists_two", "counts_two"]
    names = inputs + ["out"] + list(scratch)
    vmem = pl.BlockSpec(memory_space=pltpu.VMEM)
    hbm = pl.BlockSpec(memory_space=pl.ANY)
    return pl.pallas_call(
        functools.partial(main_kernel, d, names),
        out_shape=jax.ShapeDtypeStruct((d.piece, d.out_width), bf16),
        in_specs=[hbm, vmem, hbm, hbm, hbm, hbm, vmem, vmem, vmem, vmem],
        out_specs=vmem,
        scratch_shapes=list(scratch.values()),
        compiler_params=pltpu.CompilerParams(
            collective_id=1, has_side_effects=True, vmem_limit_bytes=60 * 1024 * 1024
        ),
    )(
        feature_table,
        hub_table,
        first_self,
        first_pooled,
        second_self,
        second_pooled,
        first_lists.T,
        first_counts[None, :],
        second_lists.T,
        second_counts[None, :],
    )


def solution(mesh):
    return jax.shard_map(
        body,
        mesh=mesh,
        in_specs=(
            P("node", "feat"),
            P("node", "feat"),
            P("feat", None),
            P("feat", None),
            P("feat", None),
            P("feat", None),
            P("node", None),
            P("node"),
            P("node", None),
            P("node"),
        ),
        out_specs=P(("node", "feat"), None),
        check_vma=False,
    )
```

time: 88.2 us -> 75.5 us (0.86)
  Pallas kernels: 81 us -> 72.6 us
  other arithmetic: 2.75 us -> 0 us
  local copies, waits for them, and re-layouts: 4.14 us -> 2.62 us
    pallas_call x1, Pallas kernels: 81 us -> 72.6 us  [body(): pl.pallas_call(functools.partial(main_kernel, d, names), out_shape=jax.Sh...]
    transpose x2 -> x0, other arithmetic: 1.45 us -> none  [the longest x1 0.74 us: body(): lists_one = jnp.where(slots_one < first_counts[:, None], first_lists, -1).T]
    concatenate x2 -> x0, other arithmetic: 1.3 us -> none  [the longest x1 0.69 us: body(): lists_two = jnp.concatenate([lists_two, second_counts[None, :]], axis=0)]
    pad x1 -> x0, local copies, waits for them, and re-layouts: 1.3 us -> none  [body(): hubs = jnp.pad(hub_table, ((0, -hubs_here % 16), (0, 0)))]
where the time goes in v1:
time: 75.5 us; the launch traced here: 75.2 us
  Pallas kernels  72.6 us (96%)
  local copies, waits for them, and re-layouts  2.62 us (3%)
    pallas_call x1, Pallas kernels, body(): pl.pallas_call(functools.partial(main_kernel, d, names), out_shape=jax.Sh...  72.6 us

profile of v1, /device:TPU:0, one launch (start us, length us, event | category | flops | bytes accessed | tf_op | source)
XLA Modules:
  0.0 75.2 jit_solution(3867115287383134690)
XLA Ops:
  0.0 1.2 %broadcast_in_dim.6.refs_7_ = s32[1,384]{1,0:T(1,128)} reshape(s32[384]{0:T(512)} %param.17) | data formatting | bytes 3072 | tf_op jit(solution)/shard_map/broadcast_in_dim | solution.py:646
  1.2 72.6 %shard_map.100 = bf16[64,256]{1,0:T(8,128)(2,1)} custom-call(bf16[1024,512]{1,0:T(8,128)(2,1)} %refs_0_.1, bf16[4,512]{1,0:T(4,128)(2,1)} %refs_1_.1, bf16[512,2048]{1,0:T(8,128)(2,1)} %refs_2_.1, bf16[512,2048]{1,0:T(8,128)(2,1)} %refs_3_.1, bf16[512,256]{1,0:T(8,128)(2,1)} %refs_4_.1, bf16[512,256]{1,0:T(8,128)(2,1)} %refs_5_.1, s32[10,384]{1,0:T(8,128)} %bitcast.3, ...), custom_call_target="tpu_custom_call" | custom-call | tf_op jit(solution)/shard_map/pallas_call | solution.py:629
  73.9 1.4 %copy.12 = bf16[64,256]{1,0:T(8,128)(2,1)} copy(bf16[64,256]{1,0:T(8,128)(2,1)} %shard_map.100) | data formatting | bytes 65536

commit v2 on v1

--- a/solution.py
+++ b/solution.py
@@ -102,7 +102,7 @@
     line = lax.broadcasted_iota(jnp.int32, (LIST_ROWS, d.front), 0)
     r.raw[...] = jnp.full((LIST_ROWS, d.front), -1, jnp.int32)
     r.raw[0 : d.fan_one, :] = r.lists_one[...]
-    counts = jnp.broadcast_to(r.counts_one[...], (LIST_ROWS, d.front))
+    counts = jnp.broadcast_to(r.counts_one[...].reshape(1, d.front), (LIST_ROWS, d.front))
     entry = jnp.where(line < jnp.minimum(counts, d.fan_one), r.raw[...], -1)
 
     def decode(to):
@@ -408,9 +408,10 @@
                 arrival(src, p).wait_recv()
                 r.acc[rows, cut] += r.z_recv[src, rows, cut].astype(f32)
 
-    early = [piece_of[q, split[0]] for q in range(d.blocks - 1)] if len(split) > 1 else []
-    for p in list(range(whole)) + early:
-        relays(p)
+    rest = [piece_of[d.blocks - 1, h] for h in split]
+    for p in range(len(pieces)):
+        if p not in rest:
+            relays(p)
     for p in range(whole):
         gather(p)
     loads[2].wait()
@@ -473,9 +474,11 @@
             p_copy(q, o).start()
 
     for q in range(d.blocks):
-        for h in split:
-            if piece_of[q, h] not in early:
-                relays(piece_of[q, h])
+        if q == d.blocks - 2:
+            relays(rest[0])
+        if q == d.blocks - 1:
+            for p in rest:
+                relays(p)
         if q > 0:
             across(q - 1)
         for h in split:
@@ -487,10 +490,11 @@
             for o in range(d.feats - 1):
                 for copy in v_copies(o):
                     copy.wait()
-        if q > 0:
-            finish(q - 1)
+    for q in range(d.blocks - 2):
+        finish(q)
     across(d.blocks - 1)
-    finish(d.blocks - 1)
+    for q in range(max(d.blocks - 2, 0), d.blocks):
+        finish(q)
     own_two = jnp.dot(r.hidden[d.step :, :].astype(bf16), r.v_self[...], preferred_element_type=f32)
     for q in range(d.blocks):
         for o in range(d.feats - 1):
@@ -643,7 +647,7 @@
         second_self,
         second_pooled,
         first_lists.T,
-        first_counts[None, :],
+        first_counts,
         second_lists.T,
         second_counts[None, :],
     )

time: 75.5 us -> 70.8 us (0.938)
  Pallas kernels: 72.6 us -> 69.2 us
  local copies, waits for them, and re-layouts: 2.62 us -> 1.38 us
    pallas_call x1, Pallas kernels: 72.6 us -> 69.2 us  [body(): pl.pallas_call(functools.partial(main_kernel, d, names), out_shape=jax.Sh...]
    broadcast_in_dim x1 -> x0, local copies, waits for them, and re-layouts: 1.24 us -> none  [body(): first_counts[None, :]]
where the time goes in v2:
time: 70.8 us; the launch traced here: 70.6 us
  Pallas kernels  69.2 us (98%)
  local copies, waits for them, and re-layouts  1.38 us (2%)
    pallas_call x1, Pallas kernels, body(): pl.pallas_call(functools.partial(main_kernel, d, names), out_shape=jax.Sh...  69.2 us

profile of v2, /device:TPU:0, one launch (start us, length us, event | category | flops | bytes accessed | tf_op | source)
XLA Modules:
  0.0 70.6 jit_solution(1581218551219596262)
XLA Ops:
  0.0 69.2 %shard_map.100 = bf16[64,256]{1,0:T(8,128)(2,1)} custom-call(bf16[1024,512]{1,0:T(8,128)(2,1)} %refs_0_.1, bf16[4,512]{1,0:T(4,128)(2,1)} %refs_1_.1, bf16[512,2048]{1,0:T(8,128)(2,1)} %refs_2_.1, bf16[512,2048]{1,0:T(8,128)(2,1)} %refs_3_.1, bf16[512,256]{1,0:T(8,128)(2,1)} %refs_4_.1, bf16[512,256]{1,0:T(8,128)(2,1)} %refs_5_.1, s32[10,384]{1,0:T(8,128)} %bitcast.3, ...), custom_call_target="tpu_custom_call" | custom-call | tf_op jit(solution)/shard_map/pallas_call | solution.py:633
  69.2 1.4 %copy.12 = bf16[64,256]{1,0:T(8,128)(2,1)} copy(bf16[64,256]{1,0:T(8,128)(2,1)} %shard_map.100) | data formatting | bytes 65536

commit v3 on v2

--- a/solution.py
+++ b/solution.py
@@ -59,9 +59,13 @@
     place = core * d.big_y + y
     x_peers = [{"node": z * d.big_x + lax.rem(x + o, d.big_x)} for o in range(1, d.big_x)]
     y_peers = [{"feat": lax.rem(y + o, d.big_y) * CORES + core} for o in range(1, d.big_y)]
-    n_peers = [{"node": lax.rem(node + o, d.shards)} for o in range(1, d.shards)]
+    z_peers = [{"node": lax.rem(z + o, d.big_z) * d.big_x + x} for o in range(1, d.big_z)]
     f_peers = [{"feat": lax.rem(feat + o, d.feats)} for o in range(1, d.feats)]
     c_peer = {"feat": y * CORES + other}
+    p_peers = []
+    for o in range(1, d.big_x * d.feats):
+        spot = lax.rem(x * d.feats + feat + o, d.big_x * d.feats)
+        p_peers.append({"node": z * d.big_x + spot // d.feats, "feat": lax.rem(spot, d.feats)})
 
     def z_peer(to):
         return {"node": to * d.big_x + x}
@@ -83,7 +87,7 @@
     r.tables[hub_top : d.depth, :] = jnp.zeros((d.depth - hub_top, d.width), bf16)
     my_hubs = pl.ds(pl.multiple_of(hub_top + x * HUB_ROWS, HUB_ROWS), HUB_ROWS)
     r.tables[my_hubs, :] = r.hubs[...]
-    greet(n_peers + f_peers)
+    greet(z_peers + p_peers)
 
     def x_copy(h, o):
         cut = pl.ds(h * LANES, LANES)
@@ -140,12 +144,12 @@
     second = jnp.where(line_two < jnp.minimum(counts_two, d.fan_two), r.raw_two[...], -1)
     second = jnp.where(line_two == d.fan_two, counts_two, second)
     r.s_send[...] = second
-    r.s_recv[node] = second
+    r.s_recv[z] = second
 
     def s_copy(o):
-        return remote(r.s_send, r.s_recv.at[node], r.s_ss.at[o], r.s_rs.at[o], n_peers[o])
-
-    for o in range(d.shards - 1):
+        return remote(r.s_send, r.s_recv.at[z], r.s_ss.at[o], r.s_rs.at[o], z_peers[o])
+
+    for o in range(d.big_z - 1):
         s_copy(o).start()
 
     for h in range(1, d.chunks):
@@ -294,8 +298,8 @@
             final_copy(s, p).start()
 
     def send_all(ps):
-        for p in ps:
-            for s in range(d.big_z - 1):
+        for s in range(d.big_z - 1):
+            for p in ps:
                 launch(s, p)
 
     def chunk(h):
@@ -306,6 +310,9 @@
             sums(h, s)
             if h < split[0]:
                 launch(s, h)
+            elif last > 1:
+                for q in range(d.blocks - 1):
+                    launch(s, piece_of[q, h])
             return carry
 
         lax.fori_loop(0, d.big_z - 1, one_target, 0)
@@ -324,11 +331,14 @@
         mine = r.turned[pl.ds(pl.multiple_of(feat * d.piece, 8), d.piece), :]
         row = pl.multiple_of(n * d.piece, 16)
 
-        def store(start, value):
-            r.matrix_two[pl.ds(row, d.piece), start : start + LANES] = value
-
-        found = jnp.clip(mine[:, 0 : d.fan_two] - node * d.front, -1, d.front)
-        count_tiles(found, d.fan_two, second_names, store)
+        for slot in range(d.big_x):
+
+            def store(start, value, base=slot * d.front):
+                r.matrix_two[pl.ds(row, d.piece), base + start : base + start + LANES] = value
+
+            owner = z * d.big_x + slot
+            found = jnp.clip(mine[:, 0 : d.fan_two] - owner * d.front, -1, d.front)
+            count_tiles(found, d.fan_two, second_names, store)
         r.scale_two[pl.ds(row, d.piece), :] = 1.0 / mine[:, d.fan_two : d.fan_two + 1].astype(f32)
         return carry
 
@@ -365,35 +375,36 @@
         return carry
 
     lax.fori_loop(0, d.big_z - 1, first_sums, 0)
-    loads[1].wait()
-    lax.fori_loop(0, TILES, own_part, 0)
+    if last == 0:
+        loads[1].wait()
+        lax.fori_loop(0, TILES, own_part, 0)
     for h in range(1, d.chunks):
         if h < last - 1:
             relays(h - 1)
+        if h == last and last > 1:
+            relays(piece_of[0, last - 1])
         chunk(h)
+        if h == 1:
+            loads[1].wait()
+            lax.fori_loop(0, TILES, own_part, 0)
         if h == last - 1:
-            if h > 0:
-                send_all([piece_of[q, h] for q in range(d.blocks - 1)])
             if h - 1 >= 0 and split[0] > h - 1:
                 relays(h - 1)
         if h == max(last - 2, 1):
-            for o in range(d.shards - 1):
+            for o in range(d.big_z - 1):
                 s_copy(o).wait()
-            lax.fori_loop(0, d.shards, fill_second, 0)
+            lax.fori_loop(0, d.big_z, fill_second, 0)
         if h == last - 1:
             fill(own_slot)
     if last <= 1:
         if last == 0:
-            for o in range(d.shards - 1):
+            for o in range(d.big_z - 1):
                 s_copy(o).wait()
-            lax.fori_loop(0, d.shards, fill_second, 0)
+            lax.fori_loop(0, d.big_z, fill_second, 0)
         fill(own_slot)
         send_all(range(whole, len(pieces)))
     else:
-        send_all([piece_of[q, last] for q in range(d.blocks - 1)])
         send_all([piece_of[d.blocks - 1, h] for h in split])
-    r.acc[...] = jnp.dot(r.matrix[own_slot], r.tables[...], preferred_element_type=f32)
-
     def gather(p):
         top, deep, h = pieces[p]
         rows = slice(top, top + deep)
@@ -409,11 +420,15 @@
                 r.acc[rows, cut] += r.z_recv[src, rows, cut].astype(f32)
 
     rest = [piece_of[d.blocks - 1, h] for h in split]
+    ahead = [piece_of[q, split[0]] for q in range(d.blocks - 1)] if len(split) > 1 else []
+    for p in list(range(whole)) + ahead:
+        relays(p)
+    r.acc[...] = jnp.dot(r.matrix[own_slot], r.tables[...], preferred_element_type=f32)
+    for p in range(whole):
+        gather(p)
     for p in range(len(pieces)):
         if p not in rest:
             relays(p)
-    for p in range(whole):
-        gather(p)
     loads[2].wait()
     half = d.big_y * d.step
 
@@ -455,9 +470,12 @@
 
         lax.fori_loop(0, TILES, tile, 0)
 
+    def proj_rows(q):
+        return pl.ds(pl.multiple_of(x * d.front + q * block + place * d.step, d.step), d.step)
+
     def p_copy(q, o):
-        at = r.proj.at[pl.ds(pl.multiple_of(q * block + place * d.step, d.step), d.step)]
-        return remote(at, at, r.p_ss.at[q, o], r.p_rs.at[q, o], f_peers[o])
+        at = r.proj.at[proj_rows(q)]
+        return remote(at, at, r.p_ss.at[q, o], r.p_rs.at[q, o], p_peers[o])
 
     def finish(q):
         mine = slice(q * d.step, (q + 1) * d.step)
@@ -468,9 +486,8 @@
                 total = total + r.y_recv[q, j, o].astype(f32)
             r.hidden[mine, j * d.tile : (j + 1) * d.tile] = jnp.maximum(total, 0.0)
         value = jnp.dot(r.hidden[mine, :].astype(bf16), r.v_pool[...], preferred_element_type=f32)
-        at = pl.ds(pl.multiple_of(q * block + place * d.step, d.step), d.step)
-        r.proj[at, :] = value.astype(bf16).astype(r.proj.dtype)
-        for o in range(d.feats - 1):
+        r.proj[proj_rows(q), :] = value.astype(bf16).astype(r.proj.dtype)
+        for o in range(len(p_peers)):
             p_copy(q, o).start()
 
     for q in range(d.blocks):
@@ -497,21 +514,21 @@
         finish(q)
     own_two = jnp.dot(r.hidden[d.step :, :].astype(bf16), r.v_self[...], preferred_element_type=f32)
     for q in range(d.blocks):
-        for o in range(d.feats - 1):
+        for o in range(len(p_peers)):
             p_copy(q, o).wait()
     r.mixed[...] = (
         jnp.dot(r.matrix_two[...], r.proj[...].astype(bf16), preferred_element_type=f32) * r.scale_two[...]
     )
 
     def m_copy(o):
-        return remote(r.m_send.at[o], r.m_recv.at[o], r.m_ss.at[o], r.m_rs.at[o], n_peers[o])
-
-    ways = sorted(range(d.shards - 1), key=lambda o: abs(o + 1 - d.shards // 2))
+        return remote(r.m_send.at[o], r.m_recv.at[o], r.m_ss.at[o], r.m_rs.at[o], z_peers[o])
+
+    ways = sorted(range(d.big_z - 1), key=lambda o: abs(o + 1 - d.big_z // 2))
     for o in ways:
-        to = pl.multiple_of(lax.rem(node + 1 + o, d.shards) * d.piece, 16)
+        to = pl.multiple_of(lax.rem(z + 1 + o, d.big_z) * d.piece, 16)
         r.m_send[o] = r.mixed[pl.ds(to, d.piece), :].astype(bf16)
         m_copy(o).start()
-    total = own_two + r.mixed[pl.ds(pl.multiple_of(node * d.piece, 16), d.piece), :]
+    total = own_two + r.mixed[pl.ds(pl.multiple_of(z * d.piece, 16), d.piece), :]
     for s in range(d.big_z - 1):
         for p in range(len(pieces)):
             final_copy(s, p).wait_send()
@@ -564,7 +581,7 @@
     d.order = order
     bf16, f32, i32, i16 = jnp.bfloat16, jnp.float32, jnp.int32, jnp.int16
     dma, vm = pltpu.SemaphoreType.DMA, pltpu.VMEM
-    zs, xs, ys, ns, fs = d.big_z - 1, d.big_x - 1, d.big_y - 1, d.shards - 1, d.feats - 1
+    zs, xs, ys, fs = d.big_z - 1, d.big_x - 1, d.big_y - 1, d.feats - 1
     count = d.chunks * d.blocks
     half = d.big_y * d.step
     kind = bf16 if d.step % 16 == 0 else f32
@@ -580,12 +597,12 @@
         l_send=vm((zs, LIST_ROWS, d.front), i16),
         l_recv=vm((d.big_z, LIST_ROWS, d.front), i16),
         s_send=vm((8, d.targets), i32),
-        s_recv=vm((d.shards, 8, d.targets), i32),
+        s_recv=vm((d.big_z, 8, d.targets), i32),
         turned=vm((d.targets, 8), i32),
         local=vm((d.big_z, d.front, LIST_ROWS), i32),
         matrix=vm((d.big_z, d.front, d.depth), bf16),
-        matrix_two=vm((d.shards * d.piece, d.front), bf16),
-        scale_two=vm((d.shards * d.piece, 1), f32),
+        matrix_two=vm((d.big_z * d.piece, d.big_x * d.front), bf16),
+        scale_two=vm((d.big_z * d.piece, 1), f32),
         part=vm((TILES, d.front, d.tile), f32),
         hold=vm((zs, d.front, d.width), f32),
         z_send=vm((zs, d.front, d.width), bf16),
@@ -599,10 +616,10 @@
         y_send=vm((d.blocks, TILES, ys, d.step, d.tile), bf16),
         y_recv=vm((d.blocks, TILES, ys, d.step, d.tile), bf16),
         hidden=vm((d.blocks * d.step, units), f32),
-        proj=vm((d.front, d.out_width), kind),
-        mixed=vm((d.shards * d.piece, d.out_width), f32),
-        m_send=vm((ns, d.piece, d.out_width), bf16),
-        m_recv=vm((ns, d.piece, d.out_width), bf16),
+        proj=vm((d.big_x * d.front, d.out_width), kind),
+        mixed=vm((d.big_z * d.piece, d.out_width), f32),
+        m_send=vm((zs, d.piece, d.out_width), bf16),
+        m_recv=vm((zs, d.piece, d.out_width), bf16),
         load=dma((5,)),
         x_ss=dma((d.chunks, xs)),
         x_rs=dma((d.chunks, xs)),
@@ -610,8 +627,8 @@
         h_rs=dma((xs,)),
         l_ss=dma((zs,)),
         l_rs=dma((zs,)),
-        s_ss=dma((ns,)),
-        s_rs=dma((ns,)),
+        s_ss=dma((zs,)),
+        s_rs=dma((zs,)),
         v_ss=dma((2, fs)),
         v_rs=dma((2, fs)),
         z_ss=dma((zs, count)),
@@ -620,10 +637,10 @@
         c_rs=dma((d.blocks, TILES)),
         y_ss=dma((d.blocks, TILES, ys)),
         y_rs=dma((d.blocks, TILES, ys)),
-        p_ss=dma((d.blocks, fs)),
-        p_rs=dma((d.blocks, fs)),
-        m_ss=dma((ns,)),
-        m_rs=dma((ns,)),
+        p_ss=dma((d.blocks, d.big_x * d.feats - 1)),
+        p_rs=dma((d.blocks, d.big_x * d.feats - 1)),
+        m_ss=dma((zs,)),
+        m_rs=dma((zs,)),
     )
     inputs = ["table", "hub", "self_one", "pool_one", "self_two", "pool_two"]
     inputs += ["lists_one", "counts_one", "lists_two", "counts_two"]

time: 70.8 us -> 69.8 us (0.986)
  Pallas kernels: 69.2 us -> 68.1 us
    pallas_call x1, Pallas kernels: 69.2 us -> 68.1 us  [body(): pl.pallas_call(functools.partial(main_kernel, d, names), out_shape=jax.Sh...]
where the time goes in v3:
time: 69.8 us; the launch traced here: 69.5 us
  Pallas kernels  68.1 us (98%)
  local copies, waits for them, and re-layouts  1.38 us (2%)
    pallas_call x1, Pallas kernels, body(): pl.pallas_call(functools.partial(main_kernel, d, names), out_shape=jax.Sh...  68.1 us

profile of v3, /device:TPU:0, one launch (start us, length us, event | category | flops | bytes accessed | tf_op | source)
XLA Modules:
  0.0 69.5 jit_solution(2589493106694892734)
XLA Ops:
  0.0 68.1 %shard_map.100 = bf16[64,256]{1,0:T(8,128)(2,1)} custom-call(bf16[1024,512]{1,0:T(8,128)(2,1)} %refs_0_.1, bf16[4,512]{1,0:T(4,128)(2,1)} %refs_1_.1, bf16[512,2048]{1,0:T(8,128)(2,1)} %refs_2_.1, bf16[512,2048]{1,0:T(8,128)(2,1)} %refs_3_.1, bf16[512,256]{1,0:T(8,128)(2,1)} %refs_4_.1, bf16[512,256]{1,0:T(8,128)(2,1)} %refs_5_.1, s32[10,384]{1,0:T(8,128)} %bitcast.3, ...), custom_call_target="tpu_custom_call" | custom-call | tf_op jit(solution)/shard_map/pallas_call | solution.py:650
  68.1 1.4 %copy.12 = bf16[64,256]{1,0:T(8,128)(2,1)} copy(bf16[64,256]{1,0:T(8,128)(2,1)} %shard_map.100) | data formatting | bytes 65536
